TPU v7x, 128 devices: a whole 4x4x4 slice. The times are simulated.
128 devices in a mesh: site: 4 (over z), blk: 16 (over x, y), charge: 2 (over core).
Axes of the slice: x: 4, y: 4, z: 4, core: 2. Of those that a mesh axis runs over, the one named last changes fastest.
Arguments:
- theta: bfloat16 [4, 64, 128, 2048], P('site', ('blk', 'charge')), may hold values from -6 to 6
- boundary_env: bfloat16 [64, 18, 128, 128], P(('blk', 'charge')), may hold values from -1 to 1
- right_env: bfloat16 [4, 64, 18, 128, 128], P('site', ('blk', 'charge')), may hold values from -1 to 1
- site_tensors: bfloat16 [4, 2, 64, 4, 128, 128], P('site', None, ('blk', 'charge')), may hold values from -0.375 to 0.375
- site_mpo: bfloat16 [4, 2, 18, 18, 4, 4], P('site'), may hold values from -0.75 to 0.75
- bond_ops: bfloat16 [4, 18, 16, 16], P('site'), may hold values from -1 to 1
- block_energy: float32 [4, 64], P('site', ('blk', 'charge')), may hold values from 1 to 4
- sector_charge: int32 [4, 64], P('site', ('blk', 'charge')), may hold values from 0 to 63, as said below
- block_len: int32 [4, 64], P('site', ('blk', 'charge')), may hold values from 64 to 128
- channel_charge: int32 [18], replicated, may hold values from -1 to 1
Outputs:
- env_out: bfloat16 [4, 64, 18, 128, 128], P('site', ('blk', 'charge'))
- lanczos: bfloat16 [4, 64, 128, 2048], P('site', ('blk', 'charge'))
- coefficients: float32 [4, 2], P('site')
Inputs may be any that keep to these rules, and one draw needn't show every extreme that they name: `sector_charge`: in each section every label of 0 to 63 appears exactly once; the blocks held at index c of the charge axis carry labels of parity c.
All inputs are finite; a program needn't handle non-finite values.
Results may differ from a plain program's by a relative error of at most 0.03.
Values may be sent and summed in bfloat16 or wider, within the bound.
A program may use at most 128 MiB of HBM per device.

v0:
```python
import jax
import jax.numpy as jnp
from jax import lax
from jax.sharding import PartitionSpec as P

BS = 128
M = 2048
NS = 64


def from_behind(block, axis, distance):
    devices = range(lax.axis_size(axis))
    route = [(i - distance, i) for i in devices if i - distance in devices]
    return lax.ppermute(block, axis, route)


def from_partner(shard, axis, bit):
    return lax.ppermute(shard, axis, [(i, i ^ 1 << bit) for i in range(lax.axis_size(axis))])


def env_update(environ, tensors, site_op):

    def one_block(entries):
        env_block, site_blocks = entries
        left_part = jnp.einsum(
            "wab,sbc->wsac", env_block, site_blocks, preferred_element_type=jnp.float32
        ).astype(jnp.bfloat16)
        mixed = jnp.einsum(
            "wvts,wsac->vtac", site_op, left_part, preferred_element_type=jnp.float32
        ).astype(jnp.bfloat16)
        return jnp.einsum(
            "tab,vtac->vbc", site_blocks, mixed, preferred_element_type=jnp.float32
        ).astype(jnp.bfloat16)

    return lax.map(one_block, (environ, tensors))


def block_product(env_block, right_blocks, chosen, ops, charges):

    def segment(total_sum, entries):
        left_block, right_block, bond_op, charge = entries
        source_tile = lax.dynamic_index_in_dim(chosen, charge + 1, 0, keepdims=False)
        contracted = jnp.dot(left_block, source_tile, preferred_element_type=jnp.float32).astype(
            jnp.bfloat16
        )
        shaped = contracted.reshape(contracted.shape[0], ops.shape[1], -1)
        applied = jnp.einsum(
            "asb,bc->asc", shaped, right_block, preferred_element_type=jnp.float32
        ).astype(jnp.bfloat16)
        final = jnp.einsum("asc,st->atc", applied, bond_op, preferred_element_type=jnp.float32)
        return (total_sum + final.reshape(total_sum.shape), None)

    start_sum = jnp.zeros((chosen.shape[1], chosen.shape[2]), jnp.float32)
    return lax.scan(segment, start_sum, (env_block, right_blocks, ops, charges))[0]


def keep_same(values):
    return values


def pair_with(environ, tensors, site_ops):
    first = env_update(environ, tensors[0], site_ops[0])
    return env_update(first, tensors[1], site_ops[1])


def picker(wanted_labels, pieces):
    sign_pair = jnp.array([-1, 1], jnp.int32)
    wanted = wanted_labels[:, None] + sign_pair[None, :]
    incoming_tiles, incoming_tags = pieces
    matches = (incoming_tags[None, None, :] == wanted[:, :, None]).astype(jnp.bfloat16)
    picked = jnp.einsum(
        "kst,tam->ksam", matches, incoming_tiles, preferred_element_type=jnp.float32
    )
    return picked.astype(jnp.bfloat16)


def on_device(
    theta,
    boundary_env,
    right_env,
    site_tensors,
    site_mpo,
    bond_ops,
    block_energy,
    sector_charge,
    block_len,
    channel_charge,
):
    section = lax.axis_index("site")
    site_count = lax.axis_size("site")
    tensors = site_tensors[0]
    site_ops = site_mpo[0]

    def update_pair(environ):
        return pair_with(environ, tensors, site_ops)

    state = boundary_env
    env_in = boundary_env
    for segment in range(site_count):
        state = lax.cond(section == segment, update_pair, keep_same, state)
        if segment + 1 < site_count:
            received = from_behind(state, "site", 1)
            is_next = section == segment + 1
            state = jnp.where(is_next, received, state)
            env_in = jnp.where(is_next, received, env_in)
    labels = sector_charge[0]
    live_rows = block_len[0]
    row_mask = jnp.arange(theta.shape[2], dtype=jnp.int32)[None, :] < live_rows[:, None]
    theta_m = theta[0] * row_mask[:, :, None].astype(jnp.bfloat16)
    other_labels = from_partner(labels, "charge", 0)
    for_other = picker(
        other_labels,
        (
            lax.all_gather(theta_m, "blk", axis=0, tiled=True),
            lax.all_gather(labels, "blk", axis=0, tiled=True),
        ),
    )
    partner = from_partner(for_other, "charge", 0)
    chosen_all = jnp.stack([partner[:, 0], theta_m, partner[:, 1]], axis=1)
    ops = bond_ops[0]

    def per_block(entries):
        return block_product(entries[0], entries[1], entries[2], ops, channel_charge)

    product = lax.map(per_block, (env_in, right_env[0], chosen_all))
    theta_f = theta_m.astype(jnp.float32)
    product = (
        product * row_mask[:, :, None].astype(jnp.float32)
        - block_energy[0][:, None, None] * theta_f
    )
    entries_count = NS * BS * M
    correlation, norm_theta = lax.psum(
        (jnp.sum(theta_f * product), jnp.sum(theta_f * theta_f)), ("blk", "charge")
    )
    rayleigh = correlation / norm_theta
    residual = product - rayleigh * theta_f
    residual_sq = lax.psum(jnp.sum(residual * residual), ("blk", "charge"))
    mean_sq = residual_sq / entries_count
    lanczos = (residual / jnp.sqrt(mean_sq + 1e-06)).astype(jnp.bfloat16)
    coefficients = jnp.stack([rayleigh, jnp.sqrt(mean_sq)])[None, :]
    return (state[None], lanczos[None], coefficients)


def solution(mesh):
    return jax.shard_map(
        on_device,
        mesh=mesh,
        in_specs=(
            P("site", ("blk", "charge"), None, None),
            P(("blk", "charge"), None, None, None),
            P("site", ("blk", "charge"), None, None, None),
            P("site", None, ("blk", "charge"), None, None, None),
            P("site", None, None, None, None, None),
            P("site", None, None, None),
            P("site", ("blk", "charge")),
            P("site", ("blk", "charge")),
            P("site", ("blk", "charge")),
            P(),
        ),
        out_specs=(
            P("site", ("blk", "charge"), None, None, None),
            P("site", ("blk", "charge"), None, None),
            P("site", None),
        ),
        check_vma=False,
    )
```

profile of v0, /device:TPU:97, one launch (start us, length us, event | category | flops | bytes accessed | tf_op | source)
XLA Modules:
  0.0 685.1 jit_solution(11959686821084895500)
XLA Ops:
  9.1 2.4 bitcast_multiply_fusion
  18.5 13.5 %all-reduce = s32[32]{0:T(128)S(1)} all-reduce(s32[32]{0:T(128)S(1)} %bitcast_dynamic-update-slice_fusion.1), channel_id=2, replica_groups=mesh['site'=4,'blk'=16,'charge'=2] {'blk'}, use_global_device_ids=true, to_apply=%add | all-reduce | flops 32 | bytes 256
  32.1 11.6 %collective-permute-done = bf16[2,18,128,128]{3,2,1,0:T(8,128)(2,1)S(1)} collective-permute-done((bf16[2,18,128,128]{3,2,1,0:T(8,128)(2,1)}, bf16[2,18,128,128]{3,2,1,0:T(8,128)(2,1)S(1)}, u32[]{:S(2)}, u32[]{:S(2)}) %collective-permute-start) | collective-permute-done | bytes 1179680 | tf_op jit(solution)/shard_map/ppermute | solution.py:14
  47.0 77.2 %all-gather.3.cloned.1.call-done = bf16[32,128,2048]{2,1,0:T(8,128)(2,1)} async-done(((bf16[2,128,2048]{2,1,0:T(8,128)(2,1)}), bf16[32,128,2048]{2,1,0:T(8,128)(2,1)}) %all-gather.3.cloned.1.call-update) | async-done | bytes 16777232 | tf_op jit(solution)/shard_map/all_gather | solution.py:114
  124.2 26.1 %fusion.233 = bf16[2,2,128,2048]{3,1,2,0:T(2,128)(2,1)} fusion(bf16[32,128,2048]{2,1,0:T(8,128)(2,1)} %all-gather.3.cloned.1.call-done, s32[32]{0:T(128)S(1)} %all-reduce, s32[2,2]{1,0:T(2,128)S(1)} %broadcast_add_fusion), kind=kOutput, calls=%fused_computation.203 | convolution fusion | flops 68157568 | bytes 18874512 | tf_op jit(solution)/shard_map/kst,tam->ksam/dot_general | solution.py:71
  151.6 9.2 %collective-permute-start.2 = (bf16[2,18,128,128]{3,2,1,0:T(8,128)(2,1)S(1)}, bf16[2,18,128,128]{3,2,1,0:T(8,128)(2,1)}, u32[]{:S(2)}, u32[]{:S(2)}) collective-permute-start(bf16[2,18,128,128]{3,2,1,0:T(8,128)(2,1)S(1)} %get-tuple-element.589), channel_id=1, source_target_pairs={{0,32},{32,64},{64,96},{1,33},{33,65},{65,97},{2,34},{34,66},{66,9... | collective-permute-start | bytes 3538952 | tf_op jit(solution)/shard_map/ppermute | solution.py:14
  162.5 2.2 copy_multiply_fusion
  164.7 85.6 %collective-permute-done.2 = bf16[2,18,128,128]{3,2,1,0:T(8,128)(2,1)} collective-permute-done((bf16[2,18,128,128]{3,2,1,0:T(8,128)(2,1)S(1)}, bf16[2,18,128,128]{3,2,1,0:T(8,128)(2,1)}, u32[]{:S(2)}, u32[]{:S(2)}) %collective-permute-start.2) | collective-permute-done | bytes 1179680 | tf_op jit(solution)/shard_map/ppermute | solution.py:14
  250.4 2.7 select_select_fusion
  253.1 5.6 fusion.247
  258.6 7.1 %pad_maximum_fusion = bf16[2,3,128,2048]{3,1,2,0:T(4,128)(2,1)S(1)} fusion(bf16[2,1,128,2048]{3,1,2,0:T(2,128)(2,1)S(1)} %get-tuple-element.724, bf16[2,1,128,2048]{3,1,2,0:T(2,128)(2,1)S(1)} %copy_multiply_fusion, bf16[2,1,128,2048]{3,1,2,0:T(2,128)(2,1)S(1)} %get-tuple-element.723), kind=kLoop, calls=%fused_computation.198 | loop fusion | flops 9437184 | bytes 6291456 | tf_op jit(solution)/shard_map/stack | solution.py:119
  265.8 3.9 copy.100
  269.7 211.9 %while.113 = (s32[]{:T(128)}, f32[2,128,2048]{2,1,0:T(8,128)}, bf16[2,18,128,128]{3,2,1,0:T(8,128)(2,1)S(1)}, bf16[2,18,128,128]{3,2,1,0:T(8,128)(2,1)}, bf16[2,...) while((s32[]{:T(128)}, f32[2,128,2048]{2,1,0:T(8,128)}, ...), condition=%wide.region_27.28_spmd, body=%wide.region_24.27_spmd.sunk | while | flops 143654912 | bytes 23926256 | solution.py:125
  269.7 2.4 dynamic-slice_bitcast_fusion.5
  272.1 2.7 dynamic-slice_bitcast_fusion.6
  274.8 99.1 %while.114 = (s32[]{:T(128)}, f32[128,2048]{1,0:T(8,128)S(1)}, bf16[18,16,16]{1,2,0:T(8,128)(2,1)}, bf16[18,128,128]{2,1,0:T(8,128)(2,1)}, s32[18]{0:T(128)S(1)}...) while((s32[]{:T(128)}, f32[128,2048]{1,0:T(8,128)S(1)}, ...), condition=%wide.region_26.26_spmd.clone, body=%wide.region_25.25_spmd.clone.sunk | while | flops 143654912 | bytes 6886593 | solution.py:54
  375.6 2.4 dynamic-slice_bitcast_fusion.5
  378.0 2.7 dynamic-slice_bitcast_fusion.6
  380.7 99.1 %while.114 = (s32[]{:T(128)}, f32[128,2048]{1,0:T(8,128)S(1)}, bf16[18,16,16]{1,2,0:T(8,128)(2,1)}, bf16[18,128,128]{2,1,0:T(8,128)(2,1)}, s32[18]{0:T(128)S(1)}...) while((s32[]{:T(128)}, f32[128,2048]{1,0:T(8,128)S(1)}, ...), condition=%wide.region_26.26_spmd.clone, body=%wide.region_25.25_spmd.clone.sunk | while | flops 143654912 | bytes 6886593 | solution.py:54
  481.5 3.8 fusion.238
  485.3 68.7 %all-reduce.1 = (f32[]{:T(128)}, f32[]{:T(128)}) all-reduce(f32[]{:T(128)} %get-tuple-element.594, f32[]{:T(128)} %get-tuple-element.593), channel_id=1, replica_groups=mesh['site'=4,'blk'=16,'charge'=2] {'blk','charge'}, use_global_device_ids=true, to_apply=%region_29.30 | all-reduce | flops 2 | bytes 16 | tf_op jit(solution)/shard_map/psum | solution.py:132
  555.4 3.3 multiply_reduce_fusion
  558.7 48.6 %conditional.7 = (bf16[1,2,18,128,128]{4,3,2,1,0:T(8,128)(2,1)}) conditional(s32[]{:T(128)} %convert_element_type.194, (bf16[2,18,128,128]{3,2,1,0:T(8,128)(2,1)S(1)}) %tuple.289, (bf16[2,2,4,128,128]{3,4,2,1,0:T(8,128)(2,1)}, bf16[2,18,18,4,4]{1,2,4,3,0:T(8,128)(2,1)}, bf16[2,18,128,128]{3,2,1,0:T(8,128)(2,1)S(1)}) %tuple.290), branch_computations={%region_18.19_spmd, %region_19.24_spmd} | conditional | flops 1553006592 | bytes 31303274 | solution.py:100
  558.7 1.9 slice_bitcast_fusion.12
  562.5 21.7 %while.109 = (s32[]{:T(128)}, bf16[2,18,128,128]{2,3,1,0:T(8,128)(2,1)S(1)}, bf16[2,4,128,128]{2,3,1,0:T(8,128)(2,1)}, bf16[2,18,128,128]{3,2,1,0:T(8,128)(2,1)S(1)}, bf16[18,18,4,4]{0,1,3,2:T(8,128)(2,1)}, /*index=5*/s32[]{:T(128)}) while((s32[]{:T(128)}, bf16[2,18,128,128]{2,3,1,0:T(8,128)(2,1)S(1)}, bf16[2,4,128,128]{2,3,1,0:T(8,128)(2,1)}, ...), condition=%wide.region_21.21_spmd, body=%wide.region_20.20_spmd.sunk | while | flops 776503296 | bytes 12768005 | solution.py:35
  564.4 7.2 %fusion.333 = bf16[18,4,128,128]{2,0,1,3:T(8,128)(2,1)S(1)} fusion(bf16[18,4,128,128,1]{2,3,0,1,4:T(8,128)(2,1)S(1)} %convert_bitcast_fusion.16, bf16[18,18,4,4]{0,1,3,2:T(8,128)(2,1)S(1)} %copy-done.20), kind=kOutput, calls=%fused_computation.133.clone.1 | convolution fusion | flops 171048960 | bytes 4728960 | tf_op jit(solution)/shard_map/cond/branch_1_fun/while/body/eval_jaxpr/wvts,wsac->vtac/dot_general | solution.py:28
  575.2 7.2 %fusion.333 = bf16[18,4,128,128]{2,0,1,3:T(8,128)(2,1)S(1)} fusion(bf16[18,4,128,128,1]{2,3,0,1,4:T(8,128)(2,1)S(1)} %convert_bitcast_fusion.16, bf16[18,18,4,4]{0,1,3,2:T(8,128)(2,1)S(1)} %copy-done.20), kind=kOutput, calls=%fused_computation.133.clone.1 | convolution fusion | flops 171048960 | bytes 4728960 | tf_op jit(solution)/shard_map/cond/branch_1_fun/while/body/eval_jaxpr/wvts,wsac->vtac/dot_general | solution.py:28
  584.4 21.3 %while.110 = (s32[]{:T(128)}, bf16[2,18,128,128]{2,3,1,0:T(8,128)(2,1)S(1)}, bf16[2,4,128,128]{2,3,1,0:T(8,128)(2,1)}, bf16[2,18,128,128]{2,3,1,0:T(8,128)(2,1)S...) while((s32[]{:T(128)}, bf16[2,18,128,128]{2,3,1,0:T(8,128)(2,1)S(1)}, ...), condition=%wide.region_23.23_spmd, body=%wide.region_22.22_spmd.sunk | while | flops 776503296 | bytes 12726505 | solution.py:35
  586.1 7.2 %fusion.341 = bf16[18,4,128,128]{2,0,1,3:T(8,128)(2,1)S(1)} fusion(bf16[18,4,128,128,1]{2,3,0,1,4:T(8,128)(2,1)S(1)} %convert_bitcast_fusion.17, bf16[18,18,4,4]{0,1,3,2:T(8,128)(2,1)S(1)} %get-tuple-element.1151), kind=kOutput, calls=%fused_computation.153.clone.1 | convolution fusion | flops 171048960 | bytes 4728960 | tf_op jit(solution)/shard_map/cond/branch_1_fun/while/body/eval_jaxpr/wvts,wsac->vtac/dot_general | solution.py:28
  596.8 7.2 %fusion.341 = bf16[18,4,128,128]{2,0,1,3:T(8,128)(2,1)S(1)} fusion(bf16[18,4,128,128,1]{2,3,0,1,4:T(8,128)(2,1)S(1)} %convert_bitcast_fusion.17, bf16[18,18,4,4]{0,1,3,2:T(8,128)(2,1)S(1)} %get-tuple-element.1151), kind=kOutput, calls=%fused_computation.153.clone.1 | convolution fusion | flops 171048960 | bytes 4728960 | tf_op jit(solution)/shard_map/cond/branch_1_fun/while/body/eval_jaxpr/wvts,wsac->vtac/dot_general | solution.py:28
  607.4 65.9 %psum.23 = f32[]{:T(128)} all-reduce(f32[]{:T(128)} %multiply_reduce_fusion), channel_id=1, replica_groups=mesh['site'=4,'blk'=16,'charge'=2] {'blk','charge'}, use_global_device_ids=true, to_apply=%region_33.34 | all-reduce | flops 1 | bytes 8 | tf_op jit(solution)/shard_map/psum | solution.py:137
  674.0 3.3 fusion.240
  (273 shorter events, 183.8 us)
Async XLA Ops:
  7.2 4.4 copy-start.18
  7.2 5.4 copy-start.17
  7.2 117.0 %all-gather.3.cloned.1.call-start = ((), (), s32[]{:S(2)}) async-start(), calls=%async_computation | async-start | bytes 17825792 | tf_op jit(solution)/shard_map/all_gather | solution.py:114
  8.6 0.5 copy-start.21
  9.1 4.5 copy-start.2
  13.6 2.3 copy-start.26
  13.6 3.4 copy-start.28
  13.6 18.4 %copy-start.25 = (s32[2]{0:T(128)S(1)}, s32[2]{0:T(128)}, u32[]{:S(2)}) copy-start(s32[2]{0:T(128)} %constant.168.clone) | copy-start | bytes 28
  14.7 29.0 %collective-permute-start = (bf16[2,18,128,128]{3,2,1,0:T(8,128)(2,1)}, bf16[2,18,128,128]{3,2,1,0:T(8,128)(2,1)S(1)}, u32[]{:S(2)}, u32[]{:S(2)}) collective-permute-start(bf16[2,18,128,128]{3,2,1,0:T(8,128)(2,1)} %get-tuple-element.585), channel_id=1, source_target_pairs={{0,32},{32,64},{64,96},{1,33},{33,65},{65,97},{2,34},{34,66},{66,9... | collective-permute-start | bytes 3538952 | tf_op jit(solution)/shard_map/ppermute | solution.py:14
  16.0 16.0 %collective-permute-start.3 = (s32[2]{0:T(128)S(1)}, s32[2]{0:T(128)S(1)}, u32[]{:S(2)}, u32[]{:S(2)}) collective-permute-start(s32[2]{0:T(128)S(1)} %bitcast.620), channel_id=1, source_target_pairs={{0,1},{1,0},{2,3},{3,2},{4,5},{5,4},{6,7},{7,6},{8,9},{9,8},{10,11... | collective-permute-start | bytes 32 | tf_op jit(solution)/shard_map/ppermute | solution.py:18
  43.7 1.8 copy-start.8
  45.6 105.5 %collective-permute-start.1 = (bf16[2,18,128,128]{3,2,1,0:T(8,128)(2,1)S(1)}, bf16[2,18,128,128]{3,2,1,0:T(8,128)(2,1)}, u32[]{:S(2)}, u32[]{:S(2)}) collective-permute-start(bf16[2,18,128,128]{3,2,1,0:T(8,128)(2,1)S(1)} %get-tuple-element.587), channel_id=1, source_target_pairs={{0,32},{32,64},{64,96},{1,33},{33,65},{65,97},{2,34},{34,66},{66,9... | collective-permute-start | bytes 3538952 | tf_op jit(solution)/shard_map/ppermute | solution.py:14
  150.3 102.7 %collective-permute-start.4 = (bf16[2,2,128,2048]{3,1,2,0:T(2,128)(2,1)}, bf16[2,2,128,2048]{3,1,2,0:T(2,128)(2,1)}, u32[]{:S(2)}, u32[]{:S(2)}) collective-permute-start(bf16[2,2,128,2048]{3,1,2,0:T(2,128)(2,1)} %fusion.233), channel_id=1, source_target_pairs={{0,1},{1,0},{2,3},{3,2},{4,5},{5,4},{6,7},{7,6},{8,9},{9,8},{10,11... | collective-permute-start | bytes 6291464 | tf_op jit(solution)/shard_map/ppermute | solution.py:18
  151.2 11.3 %copy-start = (bf16[1,2,128,2048]{3,2,1,0:T(8,128)(2,1)S(1)}, bf16[1,2,128,2048]{3,2,1,0:T(8,128)(2,1)}, u32[]{:S(2)}) copy-start(bf16[1,2,128,2048]{3,2,1,0:T(8,128)(2,1)} %param.39) | copy-start | bytes 3145732
  151.2 11.3 %copy-start.22 = (bf16[2,128]{1,0:T(2,128)(2,1)S(1)}, bf16[2,128]{1,0:T(2,128)(2,1)}, u32[]{:S(2)}) copy-start(bf16[2,128]{1,0:T(2,128)(2,1)} %copy-done.21) | copy-start | bytes 1540
  151.6 98.7 %collective-permute-start.2 = (bf16[2,18,128,128]{3,2,1,0:T(8,128)(2,1)S(1)}, bf16[2,18,128,128]{3,2,1,0:T(8,128)(2,1)}, u32[]{:S(2)}, u32[]{:S(2)}) collective-permute-start(bf16[2,18,128,128]{3,2,1,0:T(8,128)(2,1)S(1)} %get-tuple-element.589), channel_id=1, source_target_pairs={{0,32},{32,64},{64,96},{1,33},{33,65},{65,97},{2,34},{34,66},{66,9... | collective-permute-start | bytes 3538952 | tf_op jit(solution)/shard_map/ppermute | solution.py:14
  162.5 87.9 %copy-start.9 = (bf16[2,18,128,128]{3,2,1,0:T(8,128)(2,1)S(1)}, bf16[2,18,128,128]{3,2,1,0:T(8,128)(2,1)}, u32[]{:S(2)}) copy-start(bf16[2,18,128,128]{3,2,1,0:T(8,128)(2,1)} %copy-done.8) | copy-start | bytes 3538948
  265.8 3.9 copy-start.27
  269.7 211.9 %copy-start.23 = (f32[2,128]{1,0:T(2,128)S(1)}, f32[2,128]{1,0:T(2,128)}, u32[]{:S(2)}) copy-start(f32[2,128]{1,0:T(2,128)} %get-tuple-element.727) | copy-start | bytes 3076
  269.7 211.9 %copy-start.24 = (f32[1,2]{1,0:T(1,128)S(1)}, f32[1,2]{1,0:T(1,128)}, u32[]{:S(2)}) copy-start(f32[1,2]{1,0:T(1,128)} %param.45) | copy-start | bytes 28
  269.7 5.2 copy-start.4
  374.0 1.6 copy-start.5
  375.6 5.1 copy-start.4
  479.9 1.6 copy-start.5
  481.5 73.8 %copy-start.1 = (bf16[1,2,128,2048]{3,2,1,0:T(8,128)(2,1)S(1)}, bf16[1,2,128,2048]{3,2,1,0:T(8,128)(2,1)}, u32[]{:S(2)}) copy-start(bf16[1,2,128,2048]{3,2,1,0:T(8,128)(2,1)} %param.39) | copy-start | bytes 3145732
  481.5 73.8 %copy-start.3 = (bf16[2,18,128,128]{3,2,1,0:T(8,128)(2,1)S(1)}, bf16[2,18,128,128]{3,2,1,0:T(8,128)(2,1)}, u32[]{:S(2)}) copy-start(bf16[2,18,128,128]{3,2,1,0:T(8,128)(2,1)} %get-tuple-element.726) | copy-start | bytes 3538948
  562.7 1.7 copy-start.20
  564.4 7.2 %copy-start.14 = (bf16[2,4,128,128]{2,3,1,0:T(8,128)(2,1)S(1)}, bf16[2,4,128,128]{2,3,1,0:T(8,128)(2,1)}, u32[]{:S(2)}) copy-start(bf16[2,4,128,128]{2,3,1,0:T(8,128)(2,1)} %get-tuple-element.1131) | copy-start | bytes 786436 | tf_op jit(solution)/shard_map/cond/branch_1_fun/while
  573.4 1.7 copy-start.20
  575.2 7.2 %copy-start.14 = (bf16[2,4,128,128]{2,3,1,0:T(8,128)(2,1)S(1)}, bf16[2,4,128,128]{2,3,1,0:T(8,128)(2,1)}, u32[]{:S(2)}) copy-start(bf16[2,4,128,128]{2,3,1,0:T(8,128)(2,1)} %get-tuple-element.1131) | copy-start | bytes 786436 | tf_op jit(solution)/shard_map/cond/branch_1_fun/while
  586.1 7.2 %copy-start.11 = (bf16[2,4,128,128]{2,3,1,0:T(8,128)(2,1)S(1)}, bf16[2,4,128,128]{2,3,1,0:T(8,128)(2,1)}, u32[]{:S(2)}) copy-start(bf16[2,4,128,128]{2,3,1,0:T(8,128)(2,1)} %get-tuple-element.1149) | copy-start | bytes 786436 | tf_op jit(solution)/shard_map/cond/branch_1_fun/while
  596.7 7.2 %copy-start.11 = (bf16[2,4,128,128]{2,3,1,0:T(8,128)(2,1)S(1)}, bf16[2,4,128,128]{2,3,1,0:T(8,128)(2,1)}, u32[]{:S(2)}) copy-start(bf16[2,4,128,128]{2,3,1,0:T(8,128)(2,1)} %get-tuple-element.1149) | copy-start | bytes 786436 | tf_op jit(solution)/shard_map/cond/branch_1_fun/while
Sparse Core Ops, SparseCore 0:
  11.7 112.4 all-gather.2
where the time goes:
time: 698 us; the launch traced here: 685 us
  waiting for transfers between devices  174 us (25%)
  matrix products  161 us (23%)
  blocking collectives  148 us (21%)
  local copies, waits for them, and re-layouts  62.4 us (9%)
  other arithmetic  56 us (8%)
  loops' own time  52.4 us (8%)
  between operations  17.4 us (2%)
  starting transfers between devices  13.8 us (2%)
    ppermute x3, waiting for transfers between devices, from_behind(): return lax.ppermute(block, axis, route)  97.3 us
    all_gather x1, waiting for transfers between devices, on_device(): lax.all_gather(theta_m, 'blk', axis=0, tiled=True)  77.2 us
    psum x1, blocking collectives, on_device(): lax.psum((jnp.sum(theta_f * product), jnp.sum(theta_f * theta_f)), ('blk'...  68.7 us
    psum x1, blocking collectives, on_device(): residual_sq = lax.psum(jnp.sum(residual * residual), ('blk', 'charge'))  65.9 us
    another operation x2, loops' own time, block_product(): lax.scan(segment, start_sum, (env_block, right_blocks, ops, charges))[0]  51.2 us
    dot_general x36, matrix products, segment(): jnp.dot(left_block, source_tile, preferred_element_type=jnp.float32)  48.7 us
    dot_general x36, matrix products, segment(): jnp.einsum('asc,st->atc', applied, bond_op, preferred_element_type=jnp.fl...  43.4 us
    dot_general x4, matrix products, one_block(): jnp.einsum('wvts,wsac->vtac', site_op, left_part, preferred_element_type=...  28.8 us
  transfers between devices with their start and end apart: 6, of which 3 were waited for; matrix products, arithmetic and copies ran while one was open for 6% of the time, Pallas kernels for 0%

commit v1 on v0

--- a/solution.py
+++ b/solution.py
@@ -111,7 +111,9 @@
     for_other = picker(
         other_labels,
         (
-            lax.all_gather(theta_m, "blk", axis=0, tiled=True),
+            jnp.concatenate(
+                lax.all_to_all(jnp.stack([theta_m] * lax.axis_size("blk")), "blk", 0, 0), axis=0
+            ),
             lax.all_gather(labels, "blk", axis=0, tiled=True),
         ),
     )

time: 698 us -> 867 us (1.24)
  blocking collectives: 148 us -> 408 us
  waiting for transfers between devices: 174 us -> 90.4 us
  local copies, waits for them, and re-layouts: 62.4 us -> 110 us
  matrix products: 161 us -> 120 us
  between operations: 17.4 us -> 3.95 us
    unnamed x1, blocking collectives: 13.5 us -> 279 us
    all_gather x1 -> x0, waiting for transfers between devices: 77.2 us -> none  [on_device(): lax.all_gather(theta_m, 'blk', axis=0, tiled=True)]
    reshape x0 -> x1, local copies, waits for them, and re-layouts: none -> 24.9 us  [on_device(): jnp.concatenate(lax.all_to_all(jnp.stack([theta_m] * lax.axis_size('blk')...]
    dot_general x36, matrix products: 43.4 us -> 19.1 us  [segment(): jnp.einsum('asc,st->atc', applied, bond_op, preferred_element_type=jnp.fl...]
    dot_general x1, matrix products: 26.1 us -> 9.76 us  [picker(): jnp.einsum('kst,tam->ksam', matches, incoming_tiles, preferred_element_ty...]
    all_to_all x0 -> x1, local copies, waits for them, and re-layouts: none -> 15.4 us  [on_device(): lax.all_to_all(jnp.stack([theta_m] * lax.axis_size('blk')), 'blk', 0, 0)]
    another operation x2 -> x4, local copies, waits for them, and re-layouts: 0.52 us -> 15.9 us  [the longest x2 15.3 us: on_device(): jnp.stack([theta_m] * lax.axis_size('blk'))]
  transfers between devices with their start and end apart: 6 -> 6, of which waited for: 3 -> 1; matrix products, arithmetic and copies ran while one was open for 6% -> 7% of each run, Pallas kernels for 0% -> 0%
where the time goes in v1:
time: 867 us; the launch traced here: 862 us
  blocking collectives  408 us (47%)
  matrix products  120 us (14%)
  local copies, waits for them, and re-layouts  110 us (13%)
  waiting for transfers between devices  90.4 us (10%)
  other arithmetic  59 us (7%)
  loops' own time  48.7 us (6%)
  starting transfers between devices  21.5 us (2%)
    unnamed x1, blocking collectives  279 us
    ppermute x3, waiting for transfers between devices, from_behind(): return lax.ppermute(block, axis, route)  90.4 us
    psum x1, blocking collectives, on_device(): lax.psum((jnp.sum(theta_f * product), jnp.sum(theta_f * theta_f)), ('blk'...  65.5 us
    psum x1, blocking collectives, on_device(): residual_sq = lax.psum(jnp.sum(residual * residual), ('blk', 'charge'))  63.2 us
    dot_general x36, matrix products, segment(): jnp.dot(left_block, source_tile, preferred_element_type=jnp.float32)  48.7 us
    another operation x2, loops' own time, block_product(): lax.scan(segment, start_sum, (env_block, right_blocks, ops, charges))[0]  47.5 us
    dot_general x4, matrix products, one_block(): jnp.einsum('wvts,wsac->vtac', site_op, left_part, preferred_element_type=...  28.8 us
    add x36, other arithmetic, segment(): return (total_sum + final.reshape(total_sum.shape), None)  27.1 us
  transfers between devices with their start and end apart: 6, of which 1 were waited for; matrix products, arithmetic and copies ran while one was open for 7% of the time, Pallas kernels for 0%

profile of v1, /device:TPU:97, one launch (start us, length us, event | category | flops | bytes accessed | tf_op | source)
XLA Modules:
  0.0 861.9 jit_solution(17724259683448823925)
XLA Ops:
  4.8 14.3 %stack.13 = bf16[16,2,128,2048]{3,1,2,0:T(2,128)(2,1)} broadcast(bf16[2,128,2048]{2,0,1:T(2,128)(2,1)S(1)} %copy.91), dimensions={1,2,3} | broadcast | bytes 17825792 | tf_op jit(solution)/shard_map/stack | solution.py:115
  19.1 6.9 all-to-all-start
  29.6 8.4 collective-permute-start.3
  39.4 279.3 %all-reduce = s32[32]{0:T(128)S(1)} all-reduce(s32[32]{0:T(128)S(1)} %bitcast_dynamic-update-slice_fusion.1), channel_id=2, replica_groups=mesh['site'=4,'blk'=16,'charge'=2] {'blk'}, use_global_device_ids=true, to_apply=%add | all-reduce | flops 32 | bytes 256
  318.8 2.8 broadcast_select_fusion
  323.3 15.4 %copy.92 = bf16[16,2,128,2048]{3,1,0,2:T(2,128)(2,1)} copy(bf16[16,2,128,2048]{3,1,2,0:T(2,128)(2,1)} %all-to-all-done) | data formatting | bytes 33554432 | tf_op jit(solution)/shard_map/all_to_all | solution.py:115
  338.7 24.9 %reshape.183 = bf16[32,128,2048,1]{2,0,1,3:T(8,128)(2,1)} reshape(bf16[16,2,128,2048]{3,1,0,2:T(2,128)(2,1)} %copy.92) | data formatting | bytes 33554432 | tf_op jit(solution)/shard_map/reshape | solution.py:114
  363.6 9.8 %convolution_convert_fusion.2 = bf16[2,2,128,2048]{3,1,2,0:T(2,128)(2,1)} fusion(bf16[32,128,2048,1]{2,0,1,3:T(8,128)(2,1)} %reshape.183, s32[32]{0:T(128)S(1)} %all-reduce, s32[2,2]{1,0:T(2,128)S(1)} %broadcast_add_fusion), kind=kOutput, calls=%fused_computation.200 | convolution fusion | flops 68157568 | bytes 18874512 | tf_op jit(solution)/shard_map/kst,tam->ksam/dot_general | solution.py:71
  374.9 2.8 broadcast_select_fusion.1
  380.5 2.2 copy_multiply_fusion
  382.7 90.4 %collective-permute-done.2 = bf16[2,18,128,128]{3,2,1,0:T(8,128)(2,1)} collective-permute-done((bf16[2,18,128,128]{3,2,1,0:T(8,128)(2,1)}, bf16[2,18,128,128]{3,2,1,0:T(8,128)(2,1)}, u32[]{:S(2)}, u32[]{:S(2)}) %collective-permute-start.2) | collective-permute-done | bytes 1179680 | tf_op jit(solution)/shard_map/ppermute | solution.py:14
  473.1 3.2 select_select_fusion
  476.3 5.6 fusion.241
  481.9 7.1 pad_maximum_fusion
  489.0 3.9 copy.95
  492.9 180.4 %while.113 = (s32[]{:T(128)}, f32[2,128,2048]{2,1,0:T(8,128)}, bf16[2,18,128,128]{3,2,1,0:T(8,128)(2,1)}, bf16[2,18,128,128]{3,2,1,0:T(8,128)(2,1)}, bf16[2,3,12...) while((s32[]{:T(128)}, f32[2,128,2048]{2,1,0:T(8,128)}, ...), condition=%wide.region_27.28_spmd, body=%wide.region_24.27_spmd.sunk | while | flops 143654912 | bytes 14490018 | solution.py:127
  495.1 2.8 dynamic-slice_bitcast_fusion.6
  497.8 84.2 %while.114 = (s32[]{:T(128)}, f32[128,2048]{1,0:T(8,128)S(1)}, bf16[18,16,16]{1,2,0:T(8,128)(2,1)S(1)}, bf16[18,128,128]{2,1,0:T(8,128)(2,1)}, s32[18]{0:T(128)S...) while((s32[]{:T(128)}, f32[128,2048]{1,0:T(8,128)S(1)}, ...), condition=%wide.region_26.26_spmd.clone, body=%wide.region_25.25_spmd.clone.sunk | while | flops 143654912 | bytes 6887093 | solution.py:54
  585.2 2.8 dynamic-slice_bitcast_fusion.6
  588.0 84.2 %while.114 = (s32[]{:T(128)}, f32[128,2048]{1,0:T(8,128)S(1)}, bf16[18,16,16]{1,2,0:T(8,128)(2,1)S(1)}, bf16[18,128,128]{2,1,0:T(8,128)(2,1)}, s32[18]{0:T(128)S...) while((s32[]{:T(128)}, f32[128,2048]{1,0:T(8,128)S(1)}, ...), condition=%wide.region_26.26_spmd.clone, body=%wide.region_25.25_spmd.clone.sunk | while | flops 143654912 | bytes 6887093 | solution.py:54
  673.3 3.8 fusion.232
  677.1 65.5 %all-reduce.1 = (f32[]{:T(128)}, f32[]{:T(128)}) all-reduce(f32[]{:T(128)} %get-tuple-element.594, f32[]{:T(128)} %get-tuple-element.593), channel_id=1, replica_groups=mesh['site'=4,'blk'=16,'charge'=2] {'blk','charge'}, use_global_device_ids=true, to_apply=%region_29.30 | all-reduce | flops 2 | bytes 16 | tf_op jit(solution)/shard_map/psum | solution.py:134
  743.9 3.3 multiply_reduce_fusion
  747.2 46.6 %conditional.7 = (bf16[1,2,18,128,128]{4,3,2,1,0:T(8,128)(2,1)}) conditional(s32[]{:T(128)} %convert_element_type.194, (bf16[2,18,128,128]{3,2,1,0:T(8,128)(2,1)S(1)}) %tuple.287, (bf16[2,2,4,128,128]{3,4,2,1,0:T(8,128)(2,1)S(1)}, bf16[2,18,18,4,4]{1,2,4,3,0:T(8,128)(2,1)S(1)}, bf16[2,18,128,128]{3,2,1,0:T(8,128)(2,1)S(1)}) %tuple.296), branch_computations={%region_18.19_spmd, %region_19.24_spmd} | conditional | flops 1553006592 | bytes 31303258 | solution.py:100
  749.0 21.7 %while.109 = (s32[]{:T(128)}, bf16[2,18,128,128]{2,3,1,0:T(8,128)(2,1)S(1)}, bf16[2,4,128,128]{2,3,1,0:T(8,128)(2,1)}, bf16[2,18,128,128]{3,2,1,0:T(8,128)(2,1)S(1)}, bf16[18,18,4,4]{0,1,3,2:T(8,128)(2,1)}, /*index=5*/s32[]{:T(128)}) while((s32[]{:T(128)}, bf16[2,18,128,128]{2,3,1,0:T(8,128)(2,1)S(1)}, bf16[2,4,128,128]{2,3,1,0:T(8,128)(2,1)}, ...), condition=%wide.region_21.21_spmd, body=%wide.region_20.20_spmd.sunk | while | flops 776503296 | bytes 12767997 | solution.py:35
  751.0 7.2 fusion.328
  761.7 7.2 fusion.328
  770.9 21.3 %while.110 = (s32[]{:T(128)}, bf16[2,18,128,128]{2,3,1,0:T(8,128)(2,1)S(1)}, bf16[2,4,128,128]{2,3,1,0:T(8,128)(2,1)}, bf16[2,18,128,128]{2,3,1,0:T(8,128)(2,1)S...) while((s32[]{:T(128)}, bf16[2,18,128,128]{2,3,1,0:T(8,128)(2,1)S(1)}, ...), condition=%wide.region_23.23_spmd, body=%wide.region_22.22_spmd.sunk | while | flops 776503296 | bytes 12726497 | solution.py:35
  772.6 7.2 fusion.336
  783.3 7.2 fusion.336
  793.9 63.2 %psum.23 = f32[]{:T(128)} all-reduce(f32[]{:T(128)} %multiply_reduce_fusion), channel_id=1, replica_groups=mesh['site'=4,'blk'=16,'charge'=2] {'blk','charge'}, use_global_device_ids=true, to_apply=%region_33.34 | all-reduce | flops 1 | bytes 8 | tf_op jit(solution)/shard_map/psum | solution.py:139
  857.8 3.3 fusion.234
  (280 shorter events, 160.5 us)
Async XLA Ops:
  19.1 7.0 copy-start.15
  19.1 7.3 copy-start.16
  19.1 7.6 copy-start.2
  19.1 304.2 %all-to-all-start = ((bf16[16,2,128,2048]{3,1,2,0:T(2,128)(2,1)}), bf16[16,2,128,2048]{3,1,2,0:T(2,128)(2,1)}, u32[]{:S(2)}, u32[]{:S(2)}) async-start(bf16[16,2,128,2048]{3,1,2,0:T(2,128)(2,1)} %stack.13), calls=%async_computation | async-start | bytes 33554432 | tf_op jit(solution)/shard_map/all_to_all | solution.py:115
  26.3 351.4 %copy-start.5 = (bf16[1,2,2,4,128,128]{4,5,3,2,1,0:T(8,128)(2,1)}, bf16[1,2,2,4,128,128]{4,5,3,2,1,0:T(8,128)(2,1)S(1)}, u32[]{:S(2)}) copy-start(bf16[1,2,2,4,128,128]{4,5,3,2,1,0:T(8,128)(2,1)S(1)} %copy.79) | copy-start | bytes 1572868
  26.7 351.1 %copy-start.7 = (bf16[1,2,18,18,4,4]{2,3,5,4,1,0:T(8,128)(2,1)}, bf16[1,2,18,18,4,4]{2,3,5,4,1,0:T(8,128)(2,1)S(1)}, u32[]{:S(2)}) copy-start(bf16[1,2,18,18,4,4]{2,3,5,4,1,0:T(8,128)(2,1)S(1)} %copy.80) | copy-start | bytes 62212
  26.7 2.9 copy-start.23
  26.7 11.3 %copy-start.25 = (u32[128]{0:T(128)S(1)}, u32[128]{0:T(128)}, u32[]{:S(2)}) copy-start(u32[128]{0:T(128)} %constant.180) | copy-start | bytes 1540
  26.7 292.0 %copy-start.22 = (s32[2]{0:T(128)S(1)}, s32[2]{0:T(128)}, u32[]{:S(2)}) copy-start(s32[2]{0:T(128)} %constant.168.clone) | copy-start | bytes 28
  28.3 290.5 %collective-permute-start = (bf16[2,18,128,128]{3,2,1,0:T(8,128)(2,1)}, bf16[2,18,128,128]{3,2,1,0:T(8,128)(2,1)S(1)}, u32[]{:S(2)}, u32[]{:S(2)}) collective-permute-start(bf16[2,18,128,128]{3,2,1,0:T(8,128)(2,1)} %get-tuple-element.585), channel_id=1, source_target_pairs={{0,32},{32,64},{64,96},{1,33},{33,65},{65,97},{2,34},{34,66},{66,9... | collective-permute-start | bytes 3538952 | tf_op jit(solution)/shard_map/ppermute | solution.py:14
  29.6 289.1 %collective-permute-start.3 = (s32[2]{0:T(128)S(1)}, s32[2]{0:T(128)S(1)}, u32[]{:S(2)}, u32[]{:S(2)}) collective-permute-start(s32[2]{0:T(128)S(1)} %bitcast.631), channel_id=1, source_target_pairs={{0,1},{1,0},{2,3},{3,2},{4,5},{5,4},{6,7},{7,6},{8,9},{9,8},{10,11... | collective-permute-start | bytes 32 | tf_op jit(solution)/shard_map/ppermute | solution.py:18
  318.8 2.8 copy-start.9
  321.6 53.3 %collective-permute-start.1 = (bf16[2,18,128,128]{3,2,1,0:T(8,128)(2,1)}, bf16[2,18,128,128]{3,2,1,0:T(8,128)(2,1)S(1)}, u32[]{:S(2)}, u32[]{:S(2)}) collective-permute-start(bf16[2,18,128,128]{3,2,1,0:T(8,128)(2,1)} %get-tuple-element.587), channel_id=1, source_target_pairs={{0,32},{32,64},{64,96},{1,33},{33,65},{65,97},{2,34},{34,66},{66,9... | collective-permute-start | bytes 3538952 | tf_op jit(solution)/shard_map/ppermute | solution.py:14
  373.4 102.9 %collective-permute-start.4 = (bf16[2,2,128,2048]{3,1,2,0:T(2,128)(2,1)}, bf16[2,2,128,2048]{3,1,2,0:T(2,128)(2,1)}, u32[]{:S(2)}, u32[]{:S(2)}) collective-permute-start(bf16[2,2,128,2048]{3,1,2,0:T(2,128)(2,1)} %convolution_convert_fusion.2), channel_id=1, source_target_pairs={{0,1},{1,0},{2,3},{3,2},{4,5},{5,4},{6,7},{7,6},{8,9},{9,8},{10,11... | collective-permute-start | bytes 6291464 | tf_op jit(solution)/shard_map/ppermute | solution.py:18
  374.9 2.8 copy-start.11
  377.8 2.7 copy-start
  377.8 2.7 copy-start.19
  377.8 95.3 %collective-permute-start.2 = (bf16[2,18,128,128]{3,2,1,0:T(8,128)(2,1)}, bf16[2,18,128,128]{3,2,1,0:T(8,128)(2,1)}, u32[]{:S(2)}, u32[]{:S(2)}) collective-permute-start(bf16[2,18,128,128]{3,2,1,0:T(8,128)(2,1)} %get-tuple-element.589), channel_id=1, source_target_pairs={{0,32},{32,64},{64,96},{1,33},{33,65},{65,97},{2,34},{34,66},{66,9... | collective-permute-start | bytes 3538952 | tf_op jit(solution)/shard_map/ppermute | solution.py:14
  380.5 92.6 %copy-start.4 = (bf16[2,18,128,128]{3,2,1,0:T(8,128)(2,1)S(1)}, bf16[2,18,128,128]{3,2,1,0:T(8,128)(2,1)}, u32[]{:S(2)}) copy-start(bf16[2,18,128,128]{3,2,1,0:T(8,128)(2,1)} %get-tuple-element.589) | copy-start | bytes 3538948
  380.5 92.6 %copy-start.10 = (bf16[2,18,128,128]{3,2,1,0:T(8,128)(2,1)S(1)}, bf16[2,18,128,128]{3,2,1,0:T(8,128)(2,1)}, u32[]{:S(2)}) copy-start(bf16[2,18,128,128]{3,2,1,0:T(8,128)(2,1)} %copy-done.9) | copy-start | bytes 3538948
  489.0 3.9 copy-start.24
  492.9 180.4 %copy-start.20 = (f32[2,128]{1,0:T(2,128)S(1)}, f32[2,128]{1,0:T(2,128)}, u32[]{:S(2)}) copy-start(f32[2,128]{1,0:T(2,128)} %get-tuple-element.727) | copy-start | bytes 3076
  492.9 180.4 %copy-start.21 = (f32[1,2]{1,0:T(1,128)S(1)}, f32[1,2]{1,0:T(1,128)}, u32[]{:S(2)}) copy-start(f32[1,2]{1,0:T(1,128)} %param.45) | copy-start | bytes 28
  673.3 70.6 %copy-start.1 = (bf16[1,2,128,2048]{3,2,1,0:T(8,128)(2,1)S(1)}, bf16[1,2,128,2048]{3,2,1,0:T(8,128)(2,1)}, u32[]{:S(2)}) copy-start(bf16[1,2,128,2048]{3,2,1,0:T(8,128)(2,1)} %param.39) | copy-start | bytes 3145732
  673.3 70.6 %copy-start.3 = (bf16[2,18,128,128]{3,2,1,0:T(8,128)(2,1)S(1)}, bf16[2,18,128,128]{3,2,1,0:T(8,128)(2,1)}, u32[]{:S(2)}) copy-start(bf16[2,18,128,128]{3,2,1,0:T(8,128)(2,1)} %get-tuple-element.726) | copy-start | bytes 3538948
  673.3 70.6 %copy-start.6 = (bf16[1,2,2,4,128,128]{4,5,3,2,1,0:T(8,128)(2,1)S(1)}, bf16[1,2,2,4,128,128]{4,5,3,2,1,0:T(8,128)(2,1)}, u32[]{:S(2)}) copy-start(bf16[1,2,2,4,128,128]{4,5,3,2,1,0:T(8,128)(2,1)} %copy-done.5) | copy-start | bytes 1572868
  673.3 70.7 %copy-start.8 = (bf16[1,2,18,18,4,4]{2,3,5,4,1,0:T(8,128)(2,1)S(1)}, bf16[1,2,18,18,4,4]{2,3,5,4,1,0:T(8,128)(2,1)}, u32[]{:S(2)}) copy-start(bf16[1,2,18,18,4,4]{2,3,5,4,1,0:T(8,128)(2,1)} %copy-done.7) | copy-start | bytes 62212
  749.2 1.7 copy-start.17
  751.0 7.2 copy-start.14
  761.7 7.2 copy-start.14
  772.6 7.2 copy-start.12
  783.3 7.2 copy-start.12
  (2 other events, 2.2 us)
